TPU v7x, 256 devices: a whole 4x4x8 slice. The times are simulated.
256 devices in a mesh: gx: 32 (over x, z), gy: 8 (over y, core).
Axes of the slice: x: 4, y: 4, z: 8, core: 2. Of those that a mesh axis runs over, the one named last changes fastest.
Arguments:
- self_blk: float32 [512, 128, 128], P(('gx', 'gy')), may hold values from -6 to 6
- near: bfloat16 [512, 14, 512, 128], P(('gx', 'gy')), may hold values from -0.59765625 to 0.59765625
- back: bfloat16 [512, 14, 128, 512], P(('gx', 'gy')), may hold values from -0.59765625 to 0.59765625
- interp: bfloat16 [512, 128, 512], P(('gx', 'gy')), may hold values from -0.59765625 to 0.59765625
- redinv: bfloat16 [512, 512, 512], P(('gx', 'gy')), as said below
- ranks: int32 [512], P(('gx', 'gy')), may hold values from 64 to 128, as said below
- pivots: int32 [512, 128], P(('gx', 'gy')), may hold values from 0 to 511, as said below
- neighbors: int32 [512, 14], P(('gx', 'gy')), may hold values from 0 to 511, as said below
- parent: int32 [512], P(('gx', 'gy')), may hold values from 0 to 511, as said below
Outputs:
- parent_blocks: float32 [512, 128, 128], P(('gx', 'gy'))
Inputs may be any that keep to these rules, and one draw needn't show every extreme that they name: redinv is used only on a box's redundant points. `ranks`: every draw has a box of rank 128 and a box of rank 64. `pivots`: the 128 entries of a box are distinct; the first ranks[b] of them are its skeleton points, the others are redundant points. `neighbors`: box b lies on the device of linear index b // 2, gx major. A box's neighbours are distinct, never the box itself, and lie on devices of the same gy index. The entries of the 2 boxes of one device name boxes of any one device at most 4 times; in every draw and every gy index one device is named exactly 4 times by each other device of that gy index. `parent`: A permutation of the boxes that maps the 16 boxes of each gx index onto the same 16 rows.
All inputs are finite; a program needn't handle non-finite values.
Results may differ from a plain program's by a relative error of at most 0.0049.
Values may be sent and summed in bfloat16 or wider, within the bound.
A program may use at most 64 MiB of HBM per device.

v0:
```python
import jax
import jax.numpy as jnp
from jax import lax
from jax.sharding import PartitionSpec as P


def box_terms(near_b, back_b, interp_b, redinv_b, rank_b, pivot_b):
    points_count = redinv_b.shape[0]
    skel_width = pivot_b.shape[0]
    points = jnp.arange(points_count, dtype=jnp.int32)
    living = jnp.arange(skel_width, dtype=jnp.int32) < rank_b
    select = ((pivot_b[:, None] == points[None, :]) & living[:, None]).astype(jnp.bfloat16)
    redundant = 1.0 - jnp.sum(select.astype(jnp.float32), axis=0)
    coefficients = jnp.where(
        living[:, None] & (redundant[None, :] > 0.5), interp_b, jnp.zeros_like(interp_b)
    )
    placed = jnp.einsum("kp,kq->pq", coefficients, select, preferred_element_type=jnp.float32)
    compress = (redundant[:, None] * (jnp.eye(points_count, dtype=jnp.float32) - placed)).astype(
        jnp.bfloat16
    )
    halfway = jnp.dot(redinv_b, compress, preferred_element_type=jnp.float32).astype(jnp.bfloat16)
    eliminator = jnp.einsum(
        "pq,pr->qr", compress, halfway, preferred_element_type=jnp.float32
    ).astype(jnp.bfloat16)
    lifted = jnp.einsum(
        "nkp,pq->nkq", back_b, eliminator, preferred_element_type=jnp.float32
    ).astype(jnp.bfloat16)
    return -jnp.einsum("nkq,nql->nkl", lifted, near_b, preferred_element_type=jnp.float32)


def body(self_blk, near, back, interp, redinv, ranks, pivots, neighbors, parent):
    gx_count = lax.axis_size("gx")
    lane_count = lax.axis_size("gy")
    box_dev = self_blk.shape[0]
    skel_width = self_blk.shape[1]
    block_size = skel_width * skel_width
    updates = jax.vmap(box_terms)(near, back, interp, redinv, ranks, pivots)
    entry_count = box_dev * neighbors.shape[1]
    flattened = updates.reshape(entry_count, block_size)
    targets = neighbors.reshape(entry_count)
    dest_row = targets // box_dev // lane_count
    dest_slot = targets % box_dev
    spread = (
        (dest_row * box_dev + dest_slot)[:, None]
        == jnp.arange(gx_count * box_dev, dtype=jnp.int32)[None, :]
    ).astype(jnp.float32)
    outgoing = jnp.einsum("us,uk->sk", spread, flattened, precision=lax.Precision.HIGHEST).astype(
        jnp.bfloat16
    )
    incoming = lax.all_to_all(
        outgoing.reshape(gx_count, box_dev, block_size),
        "gx",
        split_axis=0,
        concat_axis=0,
        tiled=True,
    )
    summed = jnp.sum(incoming, axis=0, dtype=jnp.float32)
    living = jnp.arange(skel_width, dtype=jnp.int32)[None, :] < ranks[:, None]
    masking = living[:, :, None] & living[:, None, :]
    merged = jnp.where(masking, self_blk + summed.reshape(box_dev, skel_width, skel_width), 0.0)
    row_boxes = lane_count * box_dev
    row_start = lax.axis_index("gx") * row_boxes
    local_slot = parent - row_start
    placement = (local_slot[:, None] == jnp.arange(row_boxes, dtype=jnp.int32)[None, :]).astype(
        jnp.float32
    )
    spread_out = jnp.einsum(
        "bq,bk->qk", placement, merged.reshape(box_dev, block_size), precision=lax.Precision.HIGHEST
    )
    result = lax.psum_scatter(spread_out, "gy", scatter_dimension=0, tiled=True)
    return result.reshape(box_dev, skel_width, skel_width)


def solution(mesh):
    placed = (
        P(("gx", "gy"), None, None),
        P(("gx", "gy"), None, None, None),
        P(("gx", "gy"), None, None, None),
        P(("gx", "gy"), None, None),
        P(("gx", "gy"), None, None),
        P(("gx", "gy")),
        P(("gx", "gy"), None),
        P(("gx", "gy"), None),
        P(("gx", "gy")),
    )
    return jax.shard_map(
        body, mesh=mesh, in_specs=placed, out_specs=P(("gx", "gy"), None, None), check_vma=False
    )
```

profile of v0, /device:TPU:1, one launch (start us, length us, event | category | flops | bytes accessed | tf_op | source)
XLA Modules:
  0.0 166.5 jit_solution(3497620073145175972)
XLA Ops:
  6.5 0.8 iota_compare_fusion.4
  7.4 0.8 convert_reduce_fusion.1
  8.2 0.1 fusion.9
  8.3 1.7 %multiply_convert_fusion = bf16[2,512,512]{2,1,0:T(8,128)(2,1)S(1)} fusion(f32[512,512]{1,0:T(8,128)S(1)} %fusion.9, f32[2,512]{1,0:T(2,128)S(1)} %broadcast_subtract_fusion, bf16[2,128,512]{2,1,0:T(8,128)(2,1)} %param.12, s32[2,128]{1,0:T(2,128)} %param.15, pred[2,512]{1,0:T(4,128)(4,1)S(1)} %broadcast_compare_fusion, pred[2,128]{1,0:T(4,128)(4,1)S(1)} %iota_compare_fusion.4), kind=kOutput, calls=%fused_computation.5 | convolution fusion | flops 136314880 | bytes 2365696 | tf_op jit(solution)/shard_map/vmap(kp,kq->pq)/dot_general | solution.py:17
  10.0 2.5 %fusion.8 = bf16[2,512,512,1]{2,1,3,0:T(8,128)(2,1)} fusion(bf16[2,512,512]{2,1,0:T(8,128)(2,1)S(1)} %multiply_convert_fusion, bf16[2,512,512]{2,1,0:T(8,128)(2,1)S(1)} %copy-done), kind=kOutput, calls=%fused_computation.10 | convolution fusion | flops 1074790400 | bytes 3145728 | tf_op jit(solution)/shard_map/vmap(pq,pr->qr)/dot_general | solution.py:22
  12.5 6.5 %fusion.5 = f32[2,14,128,128]{3,2,1,0:T(8,128)S(1)} fusion(bf16[2,14,512,128]{3,2,1,0:T(8,128)(2,1)} %param.10, bf16[2,512,512,1]{2,1,3,0:T(8,128)(2,1)} %fusion.8, bf16[2,14,128,512]{3,2,1,0:T(8,128)(2,1)} %param.11), kind=kOutput, calls=%fused_computation.7 | convolution fusion | flops 2351104000 | bytes 10223616 | tf_op jit(solution)/shard_map/vmap(nkq,nql->nkl)/dot_general | solution.py:28
  19.0 0.2 pad
  19.3 0.0 copy-start.2
  19.3 1.2 copy.14
  20.5 0.1 reshape.137
  20.6 3.3 %convolution_convert_fusion = bf16[64,16384]{1,0:T(8,128)(2,1)} fusion(f32[28,16384]{1,0:T(8,128)S(1)} %bitcast.38, s32[28]{0:T(128)S(1)} %fusion.25), kind=kOutput, calls=%fused_computation | convolution fusion | flops 353371904 | bytes 3932272 | tf_op jit(solution)/shard_map/us,uk->sk/dot_general | solution.py:47
  23.9 4.4 %reshape.139 = bf16[32,2,16384]{2,1,0:T(2,128)(2,1)} reshape(bf16[64,16384]{1,0:T(8,128)(2,1)} %convolution_convert_fusion) | data formatting | bytes 4194304 | tf_op jit(solution)/shard_map/reshape | solution.py:51
  28.3 12.0 %all-to-all-start = ((bf16[32,2,16384]{2,1,0:T(2,128)(2,1)}), bf16[32,2,16384]{2,1,0:T(2,128)(2,1)S(1)}, u32[]{:S(2)}, u32[]{:S(2)}) async-start(bf16[32,2,16384]{2,1,0:T(2,128)(2,1)} %reshape.139), calls=%async_computation | async-start | bytes 4194304 | tf_op jit(solution)/shard_map/all_to_all | solution.py:50
  40.3 0.2 all-reduce.3.cloned.1.call-start
  40.6 0.0 copy-start.4
  40.6 48.6 %all-to-all-done = bf16[32,2,16384]{2,1,0:T(2,128)(2,1)S(1)} async-done(((bf16[32,2,16384]{2,1,0:T(2,128)(2,1)}), bf16[32,2,16384]{2,1,0:T(2,128)(2,1)S(1)}, u32[]{:S(2)}, u32[]{:S(2)}) %all-to-all-start) | async-done | bytes 2097184 | tf_op jit(solution)/shard_map/all_to_all | solution.py:50
  89.2 1.9 %convert_reduce_fusion = f32[2,16384]{1,0:T(2,128)S(1)} fusion(bf16[32,2,16384]{2,1,0:T(2,128)(2,1)S(1)} %all-to-all-done), kind=kLoop, calls=%fused_computation.1 | loop fusion | flops 2064384 | bytes 2228224 | tf_op jit(solution)/shard_map/reduce_sum | solution.py:57
  91.0 0.1 fusion.20
  91.2 1.8 %fusion.16 = f32[16,16384]{1,0:T(8,128)} fusion(f32[1,2,128,128]{3,2,1,0:T(8,128)S(1)} %fusion.20, s32[2]{0:T(128)S(1)} %broadcast_subtract_fusion.1), kind=kOutput, calls=%fused_computation.22 | convolution fusion | flops 6291488 | bytes 1179656 | tf_op jit(solution)/shard_map/bq,bk->qk/dot_general | solution.py:67
  92.9 0.0 all-reduce.3.cloned.1.call-update
  93.0 0.6 dynamic-slice
  94.2 63.7 %all-reduce.3.cloned.1.call-done = f32[16,16384]{1,0:T(8,128)} async-done(((f32[16,16384]{1,0:T(8,128)}), f32[16,16384]{1,0:T(8,128)}) %all-reduce.3.cloned.1.call-update) | async-done | bytes 1048592
  157.9 1.1 dynamic-slice_bitcast_fusion
  159.0 0.7 copy.24
  (12 shorter events, 0.1 us)
Async XLA Ops:
  6.5 3.5 %copy-start = (bf16[2,512,512]{2,1,0:T(8,128)(2,1)S(1)}, bf16[2,512,512]{2,1,0:T(8,128)(2,1)}, u32[]{:S(2)}) copy-start(bf16[2,512,512]{2,1,0:T(8,128)(2,1)} %param.13) | copy-start | bytes 3145732
  19.3 1.2 copy-start.2
  28.3 12.3 %copy-start.3 = (s32[2]{0:T(128)S(1)}, s32[2]{0:T(128)}, u32[]{:S(2)}) copy-start(s32[2]{0:T(128)} %param.17) | copy-start | bytes 28
  28.3 60.9 %all-to-all-start = ((bf16[32,2,16384]{2,1,0:T(2,128)(2,1)}), bf16[32,2,16384]{2,1,0:T(2,128)(2,1)S(1)}, u32[]{:S(2)}, u32[]{:S(2)}) async-start(bf16[32,2,16384]{2,1,0:T(2,128)(2,1)} %reshape.139), calls=%async_computation | async-start | bytes 4194304 | tf_op jit(solution)/shard_map/all_to_all | solution.py:50
  40.3 50.7 %copy-start.1 = (f32[2,128,128]{2,1,0:T(8,128)S(1)}, f32[2,128,128]{2,1,0:T(8,128)}, u32[]{:S(2)}) copy-start(f32[2,128,128]{2,1,0:T(8,128)} %param.9) | copy-start | bytes 393220
  40.3 117.6 %all-reduce.3.cloned.1.call-start = ((), (), s32[]{:S(2)}) async-start(), calls=%async_computation.1 | async-start | bytes 2097152
  40.6 52.4 %copy-start.4 = (u32[256]{0:T(256)S(1)}, u32[256]{0:T(256)}, u32[]{:S(2)}) copy-start(u32[256]{0:T(256)} %constant.65) | copy-start | bytes 3076
Sparse Core Ops, SparseCore 0:
  93.1 64.8 all-reduce.2
where the time goes:
time: 168 us; the launch traced here: 167 us
  waiting for transfers between devices  112 us (67%)
  matrix products  15.7 us (9%)
  between operations  14.2 us (8%)
  starting transfers between devices  12.2 us (7%)
  local copies, waits for them, and re-layouts  8.26 us (5%)
  other arithmetic  3.77 us (2%)
    unnamed x2, waiting for transfers between devices  63.8 us
    all_to_all x1, waiting for transfers between devices, body(): lax.all_to_all(outgoing.reshape(gx_count, box_dev, block_size), 'gx', spl...  48.6 us
    all_to_all x1, starting transfers between devices, body(): lax.all_to_all(outgoing.reshape(gx_count, box_dev, block_size), 'gx', spl...  12 us
    dot_general x1, matrix products, box_terms(): jnp.einsum('nkq,nql->nkl', lifted, near_b, preferred_element_type=jnp.flo...  6.5 us
    reshape x1, local copies, waits for them, and re-layouts, body(): outgoing.reshape(gx_count, box_dev, block_size)  4.38 us
    unnamed x15, local copies, waits for them, and re-layouts  3.8 us
  transfers between devices with their start and end apart: 2, of which 2 were waited for; matrix products, arithmetic and copies ran while one was open for 0% of the time, Pallas kernels for 0%

commit v1 on v0

v1 whole, which is shorter than its diff:
```python
import jax
import jax.numpy as jnp
from jax import lax
from jax.experimental import pallas as pl
from jax.experimental.pallas import tpu as pltpu
from jax.sharding import PartitionSpec as P

BF = jnp.bfloat16
F32 = jnp.float32
MESH = pl.DeviceIdType.MESH
NT = (((1,), (1,)), ((), ()))

XS, ZS, YS = 4, 8, 4
BOXES_HERE, NBR, K, PTS = 2, 14, 128, 512
ENTRIES = BOXES_HERE * NBR
HALF = K // 2


class Mail:
    def __init__(self, send_sem, recv_sem):
        self.send_sem, self.recv_sem, self.made = send_sem, recv_sem, []

    def post(self, src, dst, device):
        m = len(self.made)
        copy = pltpu.make_async_remote_copy(
            src_ref=src, dst_ref=dst, send_sem=self.send_sem.at[m],
            recv_sem=self.recv_sem.at[m], device_id=device, device_id_type=MESH)
        copy.start()
        self.made.append(copy)
        return copy


MESSAGES = 96


def make_eliminator(rank, pivot_row, interp, redinv):
    point = lax.broadcasted_iota(jnp.int32, (PTS, K), 0)
    lane = lax.broadcasted_iota(jnp.int32, (PTS, K), 1)
    select_t = jnp.where((point == pivot_row) & (lane < rank), 1.0, 0.0).astype(F32)
    skel_col = jnp.sum(select_t, axis=1, keepdims=True)
    select_t = select_t.astype(BF)
    skel_row = lax.dot_general(jnp.ones((8, K), BF), select_t, NT, preferred_element_type=F32)[0:1]
    living = lax.broadcasted_iota(jnp.int32, (K, PTS), 0) < rank
    coeff = jnp.where(living & (skel_row < 0.5), interp.astype(F32), 0.0).astype(BF)
    through = -lax.dot_general(redinv, coeff, NT, preferred_element_type=F32)
    spread = lax.dot_general(through.astype(BF), select_t, NT, preferred_element_type=F32)
    halfway = jnp.where(skel_row < 0.5, redinv.astype(F32), spread).astype(BF)
    folded = -jnp.dot(coeff, halfway, preferred_element_type=F32)
    placed = jnp.dot(select_t, folded.astype(BF), preferred_element_type=F32)
    return jnp.where(skel_col < 0.5, halfway.astype(F32), placed).astype(BF)


def kernel(self_h, near_h, back_h, interp_h, redinv_h, ranks_s, pivots_v, nbr_s, par_s,
           out_ref,
           self_v, near_v, back_v, interp_v, redinv_v, elim_v, upd_v, tab_v, tab_s,
           own_par, all_par, par_tab,
           out_a, out_b, ra2, ra1, acc_a, sa, rza, rzb, acc_b, sb, rxb, gath,
           load_sem, tab_sem, send_sem, recv_sem):
    gx, gy = lax.axis_index("gx"), lax.axis_index("gy")
    x, z = gx // ZS, gx % ZS
    y, c = gy // 2, gy % 2

    def row(dx, dz):
        return ((x + dx) % XS) * ZS + (z + dz) % ZS

    def lane(dy, dc):
        return ((y + dy) % YS) * 2 + (c + dc) % 2

    xp, xm = (row(1, 0), gy), (row(XS - 1, 0), gy)
    zp, zm = (row(0, 1), gy), (row(0, ZS - 1), gy)
    yp, ym = (gx, lane(1, 0)), (gx, lane(YS - 1, 0))
    twin = (gx, lane(0, 1))
    lanes = [(gx, lane(dy, dc)) for dy in range(YS) for dc in range(2) if dy or dc]

    barrier = pltpu.get_barrier_semaphore()
    partners = [xp, xm, zp, zm] + lanes
    for device in partners:
        pl.semaphore_signal(barrier, inc=1, device_id=device, device_id_type=MESH)

    loads = []

    def load(src, dst):
        copy = pltpu.make_async_copy(src, dst, load_sem.at[len(loads)])
        copy.start()
        loads.append(copy)
        return copy

    in_i, in_r, in_b, in_n = [], [], [], []
    for b in range(BOXES_HERE):
        in_i.append(load(interp_h.at[b], interp_v.at[b]))
        in_r.append(load(redinv_h.at[b], redinv_v.at[b]))
        in_b.append(load(back_h.at[b], back_v.at[b]))
        in_n.append(load(near_h.at[b], near_v.at[b]))
    in_s = load(self_h, self_v)

    slots = lax.broadcasted_iota(jnp.int32, (1, K), 1)
    for b in range(BOXES_HERE):
        table = jnp.full((1, K), ENTRIES, jnp.int32)
        for n in range(NBR):
            target = nbr_s[b, n]
            slot = (target // (BOXES_HERE * YS * 2)) * BOXES_HERE + target % BOXES_HERE
            table = jnp.where(slots == slot, b * NBR + n, table)
        tab_v[b:b + 1, :] = table
    for b in range(BOXES_HERE):
        own_par[b:b + 1, :] = jnp.full((1, K), par_s[b], jnp.int32)
    tab_copy = pltpu.make_async_copy(tab_v, tab_s, tab_sem.at[0])
    tab_copy.start()
    upd_v[ENTRIES] = jnp.zeros((K, K), F32)

    for b in range(BOXES_HERE):
        in_i[b].wait()
        in_r[b].wait()
        elim_v[b] = make_eliminator(ranks_s[b], pivots_v[b:b + 1, :], interp_v[b], redinv_v[b])
        in_b[b].wait()
        in_n[b].wait()

        def pair(i, carry, b=b):
            rows = back_v[b, pl.ds(2 * i, 2)].reshape(2 * K, PTS)
            lifted = jnp.dot(rows, elim_v[b], preferred_element_type=F32).astype(BF)
            for h in range(2):
                upd_v[b * NBR + 2 * i + h] = jnp.dot(
                    lifted[h * K:(h + 1) * K], near_v[b, 2 * i + h], preferred_element_type=F32)
            return carry

        lax.fori_loop(0, NBR // 2, pair, 0)

    tab_copy.wait()

    def assemble(r, carry):
        for slot in range(BOXES_HERE):
            s = BOXES_HERE * r + slot
            value = (-(upd_v[tab_s[0, s]] + upd_v[tab_s[1, s]])).astype(BF)
            if slot == 0:
                out_a[r // ZS, r % ZS] = value
            else:
                out_b[r % ZS, r // ZS] = value
        return carry

    lax.fori_loop(0, XS * ZS, assemble, 0)

    pl.semaphore_wait(barrier, len(partners))
    mail = Mail(send_sem, recv_sem)

    x1, x2, x3 = (x + 1) % XS, (x + 2) % XS, (x + 3) % XS
    lo, hi = pl.ds(0, ZS // 2), pl.ds(ZS // 2, ZS // 2)
    a2p = mail.post(out_a.at[x2, lo], ra2.at[0], xp)
    a2m = mail.post(out_a.at[x2, hi], ra2.at[1], xm)

    ha, hb = pl.ds(0, XS // 2), pl.ds(XS // 2, XS // 2)
    halves = (ha, hb)

    def post_b(d, h, k):
        target = (z + k) % ZS if d == 0 else (z + ZS - k) % ZS
        return mail.post(out_b.at[target, halves[h]], rzb.at[d, h, k - 1], zp if d == 0 else zm)

    def fold_b(d, h, k):
        target = (z + k) % ZS if d == 0 else (z + ZS - k) % ZS
        out_b[target, halves[h]] = out_b[target, halves[h]] + rzb[d, h, k]

    far = {}
    far[0, 0, 4] = post_b(0, 0, 4)
    far[1, 1, 4] = post_b(1, 1, 4)
    far[0, 1, 3] = post_b(0, 1, 3)
    far[1, 0, 3] = post_b(1, 0, 3)
    a1p = [mail.post(out_a.at[x1, hi], ra1.at[0, hi], xp)]
    a1m = [mail.post(out_a.at[x3, lo], ra1.at[1, lo], xm)]

    par_home = all_par.at[gy]
    own_copy = pltpu.make_async_copy(own_par, par_home, tab_sem.at[1])
    own_copy.start()
    par_mail = [mail.post(own_par, all_par.at[gy], device) for device in lanes]

    def hop_b(k):
        for d in range(2):
            h = d
            far[d, h, k + 1].wait_recv()
            fold_b(d, h, k)
            far[d, h, k] = post_b(d, h, k)
        if k > 1:
            for d in range(2):
                h = 1 - d
                far[d, h, k].wait_recv()
                fold_b(d, h, k - 1)
                far[d, h, k - 1] = post_b(d, h, k - 1)

    hop_b(3)

    a2p.wait_recv()
    out_a[x1, lo] = out_a[x1, lo] + ra2[0]
    a1p.append(mail.post(out_a.at[x1, lo], ra1.at[0, lo], xp))
    a2m.wait_recv()
    out_a[x3, hi] = out_a[x3, hi] + ra2[1]
    a1m.append(mail.post(out_a.at[x3, hi], ra1.at[1, hi], xm))

    hop_b(2)
    hop_b(1)

    for copy in a1p + a1m:
        copy.wait_recv()
    acc_a[...] = out_a[x].astype(F32) + ra1[0].astype(F32) + ra1[1].astype(F32)

    top, bottom = pl.ds(0, HALF), pl.ds(HALF, HALF)
    part = (top, bottom)

    def target_z(d, k):
        return (z + k) % ZS if d == 0 else (z + ZS - k) % ZS

    near_a = {}
    for d in range(2):
        sa[d, 3, part[d]] = acc_a[target_z(d, 4), part[d]].astype(BF)
        near_a[d, 4] = mail.post(sa.at[d, 3, part[d]], rza.at[d, 3, part[d]], zp if d == 0 else zm)

    def hop_a(k):
        for d in range(2):
            near_a[d, k + 1].wait_recv()
            t = target_z(d, k)
            if k == 3:
                sa[d, 2, part[d]] = (acc_a[t, part[d]] + rza[d, 3, part[d]].astype(F32)).astype(BF)
                sa[d, 2, part[1 - d]] = acc_a[t, part[1 - d]].astype(BF)
            else:
                sa[d, k - 1] = (acc_a[t] + rza[d, k].astype(F32)).astype(BF)
            near_a[d, k] = mail.post(sa.at[d, k - 1], rza.at[d, k - 1], zp if d == 0 else zm)

    for d in range(2):
        for h in range(2):
            far[d, h, 1].wait_recv()
    for h in range(2):
        acc_b[halves[h]] = (out_b[z, halves[h]].astype(F32) + rzb[0, h, 0].astype(F32)
                            + rzb[1, h, 0].astype(F32))

    def target_x(d, k):
        return (x + k) % XS if d == 0 else (x + XS - k) % XS

    near_b = {}
    for d in range(2):
        sb[d, 1, part[d]] = acc_b[target_x(d, 2), part[d]].astype(BF)
        near_b[d, 2] = mail.post(sb.at[d, 1, part[d]], rxb.at[d, 1, part[d]], xp if d == 0 else xm)

    hop_a(3)
    for d in range(2):
        near_b[d, 2].wait_recv()
        t = target_x(d, 1)
        sb[d, 0, part[d]] = (acc_b[t, part[d]] + rxb[d, 1, part[d]].astype(F32)).astype(BF)
        sb[d, 0, part[1 - d]] = acc_b[t, part[1 - d]].astype(BF)
        near_b[d, 1] = mail.post(sb.at[d, 0], rxb.at[d, 0], xp if d == 0 else xm)
    hop_a(2)

    in_s.wait()
    j = lax.broadcasted_iota(jnp.int32, (K, K), 0)
    l = lax.broadcasted_iota(jnp.int32, (K, K), 1)

    def finish(slot, total):
        rank = ranks_s[slot]
        merged = jnp.where((j < rank) & (l < rank), self_v[slot] + total, 0.0)
        gath[gy, slot] = merged.astype(BF)

    here = [gy, lane(YS - 1, 0), lane(1, 0), lane(2, 0)]

    def share(slot):
        return [mail.post(gath.at[gy, slot], gath.at[gy, slot], device) for device in (yp, ym, twin)]

    def forward(slot, sent):
        got = [sent[2]]
        sent[0].wait_recv()
        far_top = mail.post(gath.at[here[1], slot, top], gath.at[here[1], slot, top], yp)
        got.append(mail.post(gath.at[here[1], slot], gath.at[here[1], slot], twin))
        sent[1].wait_recv()
        far_bottom = mail.post(gath.at[here[2], slot, bottom], gath.at[here[2], slot, bottom], ym)
        got.append(mail.post(gath.at[here[2], slot], gath.at[here[2], slot], twin))
        return got, far_top, far_bottom

    def finish_forward(slot, state):
        got, far_top, far_bottom = state
        far_top.wait_recv()
        got.append(mail.post(gath.at[here[3], slot, top], gath.at[here[3], slot, top], twin))
        far_bottom.wait_recv()
        got.append(mail.post(gath.at[here[3], slot, bottom], gath.at[here[3], slot, bottom], twin))
        return got

    for d in range(2):
        near_b[d, 1].wait_recv()
    finish(1, acc_b[x] + rxb[0, 0].astype(F32) + rxb[1, 0].astype(F32))
    sent_b = share(1)
    hop_a(1)
    state_b = forward(1, sent_b)
    for d in range(2):
        near_a[d, 1].wait_recv()
    finish(0, acc_a[z] + rza[0, 0].astype(F32) + rza[1, 0].astype(F32))
    sent_a = share(0)
    got = finish_forward(1, state_b)
    state_a = forward(0, sent_a)

    own_copy.wait()
    for copy in par_mail:
        copy.wait_recv()
    par_copy = pltpu.make_async_copy(all_par, par_tab, tab_sem.at[2])
    par_copy.start()

    got += finish_forward(0, state_a)
    par_copy.wait()
    for copy in got:
        copy.wait_recv()
    first_row = gx * (YS * 2 * BOXES_HERE) + gy * BOXES_HERE
    for q in range(BOXES_HERE):
        found_lane, found_slot = jnp.int32(0), jnp.int32(0)
        for k in range(YS * 2):
            for s in range(BOXES_HERE):
                hit = par_tab[k, s, 0] == first_row + q
                found_lane = jnp.where(hit, k, found_lane)
                found_slot = jnp.where(hit, s, found_slot)
        out_ref[q] = gath[found_lane, found_slot].astype(F32)
    for copy in mail.made:
        copy.wait_send()


def body(self_blk, near, back, interp, redinv, ranks, pivots, neighbors, parent):
    hbm = pl.BlockSpec(memory_space=pl.ANY)
    smem = pl.BlockSpec(memory_space=pltpu.SMEM)
    vmem = pl.BlockSpec(memory_space=pltpu.VMEM)
    blk = (K, K)
    return pl.pallas_call(
        kernel,
        out_shape=jax.ShapeDtypeStruct((BOXES_HERE, K, K), F32),
        in_specs=[hbm] * 5 + [smem, vmem, smem, smem],
        out_specs=vmem,
        scratch_shapes=[
            pltpu.VMEM((BOXES_HERE,) + blk, F32),
            pltpu.VMEM((BOXES_HERE, NBR, PTS, K), BF),
            pltpu.VMEM((BOXES_HERE, NBR, K, PTS), BF),
            pltpu.VMEM((BOXES_HERE, K, PTS), BF),
            pltpu.VMEM((BOXES_HERE, PTS, PTS), BF),
            pltpu.VMEM((BOXES_HERE, PTS, PTS), BF),
            pltpu.VMEM((ENTRIES + 1,) + blk, F32),
            pltpu.VMEM((BOXES_HERE, K), jnp.int32),
            pltpu.SMEM((BOXES_HERE, K), jnp.int32),
            pltpu.VMEM((BOXES_HERE, K), jnp.int32),
            pltpu.VMEM((YS * 2, BOXES_HERE, K), jnp.int32),
            pltpu.SMEM((YS * 2, BOXES_HERE, K), jnp.int32),
            pltpu.VMEM((XS, ZS) + blk, BF),
            pltpu.VMEM((ZS, XS) + blk, BF),
            pltpu.VMEM((2, ZS // 2) + blk, BF),
            pltpu.VMEM((2, ZS) + blk, BF),
            pltpu.VMEM((ZS,) + blk, F32),
            pltpu.VMEM((2, 4) + blk, BF),
            pltpu.VMEM((2, 4) + blk, BF),
            pltpu.VMEM((2, 2, 4, XS // 2) + blk, BF),
            pltpu.VMEM((XS,) + blk, F32),
            pltpu.VMEM((2, 2) + blk, BF),
            pltpu.VMEM((2, 2) + blk, BF),
            pltpu.VMEM((YS * 2, BOXES_HERE) + blk, BF),
            pltpu.SemaphoreType.DMA((9,)),
            pltpu.SemaphoreType.DMA((3,)),
            pltpu.SemaphoreType.DMA((MESSAGES,)),
            pltpu.SemaphoreType.DMA((MESSAGES,)),
        ],
        compiler_params=pltpu.CompilerParams(
            collective_id=0, has_side_effects=True, vmem_limit_bytes=48 << 20),
    )(self_blk, near, back, interp, redinv, ranks, pivots, neighbors, parent)


def solution(mesh):
    wide = ("gx", "gy")
    placed = (
        P(wide, None, None),
        P(wide, None, None, None),
        P(wide, None, None, None),
        P(wide, None, None),
        P(wide, None, None),
        P(wide),
        P(wide, None),
        P(wide, None),
        P(wide),
    )
    return jax.shard_map(
        body, mesh=mesh, in_specs=placed, out_specs=P(wide, None, None), check_vma=False
    )
```

time: 168 us -> 62.5 us (0.37)
  waiting for transfers between devices: 112 us -> 0 us
  Pallas kernels: 0 us -> 53.8 us
  matrix products: 15.7 us -> 0 us
  between operations: 14.2 us -> 0.02 us
  starting transfers between devices: 12.2 us -> 0 us
  other arithmetic: 3.77 us -> 0 us
    unnamed x2 -> x0, waiting for transfers between devices: 63.8 us -> none
    pallas_call x0 -> x1, Pallas kernels: none -> 53.8 us  [body(): pl.pallas_call(kernel, out_shape=jax.ShapeDtypeStruct((BOXES_HERE, K, K),...]
    all_to_all x1 -> x0, waiting for transfers between devices: 48.6 us -> none  [body(): lax.all_to_all(outgoing.reshape(gx_count, box_dev, block_size), 'gx', spl...]
    dot_general x5 -> x0, matrix products: 15.7 us -> none  [the longest x1 6.5 us: box_terms(): jnp.einsum('nkq,nql->nkl', lifted, near_b, preferred_element_type=jnp.flo...]
    all_to_all x1 -> x0, starting transfers between devices: 12 us -> none  [body(): lax.all_to_all(outgoing.reshape(gx_count, box_dev, block_size), 'gx', spl...]
    unnamed x15 -> x17, local copies, waits for them, and re-layouts: 3.8 us -> 8.44 us
    reshape x2 -> x0, local copies, waits for them, and re-layouts: 4.46 us -> none  [the longest x1 4.38 us: body(): outgoing.reshape(gx_count, box_dev, block_size)]
    reduce_sum x2 -> x0, other arithmetic: 2.71 us -> none  [the longest x1 1.86 us: body(): summed = jnp.sum(incoming, axis=0, dtype=jnp.float32)]
  transfers between devices with their start and end apart: 2 -> 0, of which waited for: 2 -> 0; matrix products, arithmetic and copies ran while one was open for 0% -> 0% of each run, Pallas kernels for 0% -> 0%
where the time goes in v1:
time: 62.5 us; the launch traced here: 62.3 us
  Pallas kernels  53.8 us (86%)
  local copies, waits for them, and re-layouts  8.44 us (14%)
    pallas_call x1, Pallas kernels, body(): pl.pallas_call(kernel, out_shape=jax.ShapeDtypeStruct((BOXES_HERE, K, K),...  53.8 us
    unnamed x17, local copies, waits for them, and re-layouts  8.44 us

profile of v1, /device:TPU:1, one launch (start us, length us, event | category | flops | bytes accessed | tf_op | source)
XLA Modules:
  0.0 62.3 jit_solution(5261737308962847424)
XLA Ops:
  0.0 0.0 copy-start
  0.0 2.0 %copy-done = bf16[2,14,512,128]{3,2,1,0:T(8,128)(2,1)S(1)} copy-done((bf16[2,14,512,128]{3,2,1,0:T(8,128)(2,1)S(1)}, bf16[2,14,512,128]{3,2,1,0:T(8,128)(2,1)}, u32[]{:S(2)}) %copy-start) | copy-done | bytes 3670040
  2.0 0.0 copy-start.1
  2.0 1.2 %copy-done.1 = bf16[2,512,512]{2,1,0:T(8,128)(2,1)S(1)} copy-done((bf16[2,512,512]{2,1,0:T(8,128)(2,1)S(1)}, bf16[2,512,512]{2,1,0:T(8,128)(2,1)}, u32[]{:S(2)}) %copy-start.1) | copy-done | bytes 1048600
  3.3 0.0 copy-start.2
  3.3 0.9 %copy-done.2 = bf16[2,128,512]{2,1,0:T(8,128)(2,1)S(1)} copy-done((bf16[2,128,512]{2,1,0:T(8,128)(2,1)S(1)}, bf16[2,128,512]{2,1,0:T(8,128)(2,1)}, u32[]{:S(2)}) %copy-start.2) | copy-done | bytes 262168
  4.2 0.0 copy-start.3
  4.2 0.9 %copy-done.3 = f32[2,128,128]{2,1,0:T(8,128)S(1)} copy-done((f32[2,128,128]{2,1,0:T(8,128)S(1)}, f32[2,128,128]{2,1,0:T(8,128)}, u32[]{:S(2)}) %copy-start.3) | copy-done | bytes 131096
  5.1 0.0 copy-start.4
  5.1 0.7 %copy-done.4 = s32[2,128]{1,0:T(2,128)S(1)} copy-done((s32[2,128]{1,0:T(2,128)S(1)}, s32[2,128]{1,0:T(2,128)}, u32[]{:S(2)}) %copy-start.4) | copy-done | bytes 1048
  5.8 0.0 copy-start.5
  5.8 0.7 %copy-done.5 = s32[2,14]{1,0:T(2,128)S(1)} copy-done((s32[2,14]{1,0:T(2,128)S(1)}, s32[2,14]{1,0:T(2,128)}, u32[]{:S(2)}) %copy-start.5) | copy-done | bytes 136
  6.5 0.0 copy-start.6
  6.5 0.7 %copy-done.6 = s32[2]{0:T(128)S(1)} copy-done((s32[2]{0:T(128)S(1)}, s32[2]{0:T(128)}, u32[]{:S(2)}) %copy-start.6) | copy-done | bytes 32
  7.1 0.0 copy-start.7
  7.1 0.7 %copy-done.7 = s32[2]{0:T(128)S(1)} copy-done((s32[2]{0:T(128)S(1)}, s32[2]{0:T(128)}, u32[]{:S(2)}) %copy-start.7) | copy-done | bytes 32
  7.8 53.8 %shard_map.91 = f32[2,128,128]{2,1,0:T(8,128)S(1)} custom-call(f32[2,128,128]{2,1,0:T(8,128)S(1)} %copy-done.3, bf16[2,14,512,128]{3,2,1,0:T(8,128)(2,1)S(1)} %copy-done, bf16[2,14,128,512]{3,2,1,0:T(8,128)(2,1)} %back_h.1, bf16[2,128,512]{2,1,0:T(8,128)(2,1)S(1)} %copy-done.2, bf16[2,512,512]{2,1,0:T(8,128)(2,1)S(1)} %copy-done.1, s32[2]{0:T(128)S(1)} %copy-done.6, ...), custom_call_target="tpu_custom_call" | custom-call | tf_op jit(solution)/shard_map/pallas_call | solution.py:321
  61.6 0.7 %copy.11 = f32[2,128,128]{2,1,0:T(8,128)} copy(f32[2,128,128]{2,1,0:T(8,128)S(1)} %shard_map.91) | data formatting | bytes 262144
Async XLA Ops:
  0.0 2.0 %copy-start = (bf16[2,14,512,128]{3,2,1,0:T(8,128)(2,1)S(1)}, bf16[2,14,512,128]{3,2,1,0:T(8,128)(2,1)}, u32[]{:S(2)}) copy-start(bf16[2,14,512,128]{3,2,1,0:T(8,128)(2,1)} %near_h.1) | copy-start | bytes 11010052
  2.0 1.2 %copy-start.1 = (bf16[2,512,512]{2,1,0:T(8,128)(2,1)S(1)}, bf16[2,512,512]{2,1,0:T(8,128)(2,1)}, u32[]{:S(2)}) copy-start(bf16[2,512,512]{2,1,0:T(8,128)(2,1)} %redinv_h.1) | copy-start | bytes 3145732
  3.3 0.9 %copy-start.2 = (bf16[2,128,512]{2,1,0:T(8,128)(2,1)S(1)}, bf16[2,128,512]{2,1,0:T(8,128)(2,1)}, u32[]{:S(2)}) copy-start(bf16[2,128,512]{2,1,0:T(8,128)(2,1)} %interp_h.1) | copy-start | bytes 786436
  4.2 0.9 %copy-start.3 = (f32[2,128,128]{2,1,0:T(8,128)S(1)}, f32[2,128,128]{2,1,0:T(8,128)}, u32[]{:S(2)}) copy-start(f32[2,128,128]{2,1,0:T(8,128)} %self_h.1) | copy-start | bytes 393220
  5.1 0.7 %copy-start.4 = (s32[2,128]{1,0:T(2,128)S(1)}, s32[2,128]{1,0:T(2,128)}, u32[]{:S(2)}) copy-start(s32[2,128]{1,0:T(2,128)} %pivots_v.1) | copy-start | bytes 3076
  5.8 0.7 %copy-start.5 = (s32[2,14]{1,0:T(2,128)S(1)}, s32[2,14]{1,0:T(2,128)}, u32[]{:S(2)}) copy-start(s32[2,14]{1,0:T(2,128)} %nbr_s.1) | copy-start | bytes 340
  6.5 0.7 %copy-start.6 = (s32[2]{0:T(128)S(1)}, s32[2]{0:T(128)}, u32[]{:S(2)}) copy-start(s32[2]{0:T(128)} %ranks_s.1) | copy-start | bytes 28
  7.1 0.7 %copy-start.7 = (s32[2]{0:T(128)S(1)}, s32[2]{0:T(128)}, u32[]{:S(2)}) copy-start(s32[2]{0:T(128)} %par_s.1) | copy-start | bytes 28

commit v2 on v1

v2 whole, which is shorter than its diff:
```python
import jax
import jax.numpy as jnp
from jax import lax
from jax.experimental import pallas as pl
from jax.experimental.pallas import tpu as pltpu
from jax.sharding import PartitionSpec as P

BF = jnp.bfloat16
F32 = jnp.float32
MESH = pl.DeviceIdType.MESH
NT = (((1,), (1,)), ((), ()))

XS, ZS, YS = 4, 8, 4
BOXES_HERE, NBR, K, PTS = 2, 14, 128, 512
ENTRIES = BOXES_HERE * NBR
GROUP = 2


class Mail:
    def __init__(self, send_sem, recv_sem):
        self.send_sem, self.recv_sem, self.made = send_sem, recv_sem, []

    def post(self, src, dst, device):
        m = len(self.made)
        copy = pltpu.make_async_remote_copy(
            src_ref=src, dst_ref=dst, send_sem=self.send_sem.at[m],
            recv_sem=self.recv_sem.at[m], device_id=device, device_id_type=MESH)
        copy.start()
        self.made.append(copy)
        return copy


MESSAGES = 96
VMEM_LIMIT = 62 << 20


def make_eliminator(rank, pivot_row, interp, redinv):
    point = lax.broadcasted_iota(jnp.int32, (PTS, K), 0)
    lane = lax.broadcasted_iota(jnp.int32, (PTS, K), 1)
    select_t = jnp.where((point == pivot_row) & (lane < rank), 1.0, 0.0).astype(F32)
    skel_col = jnp.sum(select_t, axis=1, keepdims=True)
    select_t = select_t.astype(BF)
    skel_row = lax.dot_general(jnp.ones((8, K), BF), select_t, NT, preferred_element_type=F32)[0:1]
    living = lax.broadcasted_iota(jnp.int32, (K, PTS), 0) < rank
    coeff = jnp.where(living & (skel_row < 0.5), interp.astype(F32), 0.0).astype(BF)
    through = -lax.dot_general(redinv, coeff, NT, preferred_element_type=F32)
    spread = lax.dot_general(through.astype(BF), select_t, NT, preferred_element_type=F32)
    halfway = jnp.where(skel_row < 0.5, redinv.astype(F32), spread).astype(BF)
    folded = -jnp.dot(coeff, halfway, preferred_element_type=F32)
    placed = jnp.dot(select_t, folded.astype(BF), preferred_element_type=F32)
    return jnp.where(skel_col < 0.5, halfway.astype(F32), placed).astype(BF)


def kernel(self_h, near_h, back_h, interp_h, redinv_h, ranks_s, pivots_v, nbr_s, par_s,
           out_ref,
           self_v, near_v, back_v, interp_v, redinv_v, elim_v, upd_v, tab_v, tab_s,
           own_par, all_par, par_tab,
           out_a, out_b, rxa, sza, rza, acc_a, rzb, sxb, rxb, acc_b, gath,
           load_sem, tab_sem, send_sem, recv_sem):
    gx, gy = lax.axis_index("gx"), lax.axis_index("gy")
    x, z = gx // ZS, gx % ZS
    y, c = gy // 2, gy % 2

    def row(dx, dz):
        return ((x + dx) % XS) * ZS + (z + dz) % ZS

    def lane(dy, dc):
        return ((y + dy) % YS) * 2 + (c + dc) % 2

    zp, zm = (row(0, 1), gy), (row(0, ZS - 1), gy)
    twin = (gx, lane(0, 1))
    lanes = [(gx, lane(dy, dc)) for dy in range(YS) for dc in range(2) if dy or dc]

    barrier = pltpu.get_barrier_semaphore()
    partners = ([(row(dx, 0), gy) for dx in range(1, XS)]
                + [(row(0, dz), gy) for dz in range(1, ZS)] + lanes)
    for device in partners:
        pl.semaphore_signal(barrier, inc=1, device_id=device, device_id_type=MESH)

    loads = []

    def load(src, dst):
        copy = pltpu.make_async_copy(src, dst, load_sem.at[len(loads)])
        copy.start()
        loads.append(copy)
        return copy

    in_i, in_r, in_b, in_n = [], [], [], []
    for b in range(BOXES_HERE):
        in_i.append(load(interp_h.at[b], interp_v.at[b]))
        in_r.append(load(redinv_h.at[b], redinv_v.at[b]))
        in_b.append(load(back_h.at[b], back_v.at[b]))
        in_n.append(load(near_h.at[b], near_v.at[b]))
    in_s = load(self_h, self_v)

    slots = lax.broadcasted_iota(jnp.int32, (1, K), 1)
    for b in range(BOXES_HERE):
        table = jnp.full((1, K), ENTRIES, jnp.int32)
        for n in range(NBR):
            target = nbr_s[b, n]
            slot = (target // (BOXES_HERE * YS * 2)) * BOXES_HERE + target % BOXES_HERE
            table = jnp.where(slots == slot, b * NBR + n, table)
        tab_v[b:b + 1, :] = table
    for b in range(BOXES_HERE):
        own_par[b:b + 1, :] = jnp.full((1, K), par_s[b], jnp.int32)
    tab_copy = pltpu.make_async_copy(tab_v, tab_s, tab_sem.at[0])
    tab_copy.start()
    upd_v[ENTRIES] = jnp.zeros((K, K), F32)

    for b in range(BOXES_HERE):
        in_i[b].wait()
        in_r[b].wait()
        elim_v[b] = make_eliminator(ranks_s[b], pivots_v[b:b + 1, :], interp_v[b], redinv_v[b])
        in_b[b].wait()
        in_n[b].wait()

        def pair(i, carry, b=b):
            rows = back_v[b, pl.ds(2 * i, 2)].reshape(2 * K, PTS)
            lifted = jnp.dot(rows, elim_v[b], preferred_element_type=F32).astype(BF)
            for h in range(2):
                upd_v[b * NBR + 2 * i + h] = jnp.dot(
                    lifted[h * K:(h + 1) * K], near_v[b, 2 * i + h], preferred_element_type=F32)
            return carry

        lax.fori_loop(0, NBR // 2, pair, 0)

    tab_copy.wait()

    def assemble(r, carry):
        kx, p = r // ZS, r % ZS
        kz = lax.select(p % 2 == 0, ZS // 2 + p // 2, ZS // 2 - 1 - p // 2)
        there = ((x + kx) % XS) * ZS + (z + kz) % ZS
        for slot in range(BOXES_HERE):
            s = BOXES_HERE * there + slot
            value = (-(upd_v[tab_s[0, s]] + upd_v[tab_s[1, s]])).astype(BF)
            if slot == 0:
                out_a[kx, p] = value
            else:
                out_b[kz, kx] = value
        return carry

    lax.fori_loop(0, XS * ZS, assemble, 0)

    pl.semaphore_wait(barrier, len(partners))
    mail = Mail(send_sem, recv_sem)

    hop = {}

    def post_b(d, h, k):
        hop[d, h, k] = mail.post(out_b.at[k if d == 0 else ZS - k, h], rzb.at[d, h, k - 1],
                                 zp if d == 0 else zm)

    def pass_b(d, h, k):
        hop[d, h, k + 1].wait_recv()
        t = k if d == 0 else ZS - k
        out_b[t, h] = out_b[t, h] + rzb[d, h, k]
        post_b(d, h, k)

    long_way = [(0, 0), (1, 2), (0, 1), (1, 3)]
    short_way = [(0, 2), (1, 0), (0, 3), (1, 1)]

    cross = {}

    def post_a(g):
        span = pl.ds(g * GROUP, GROUP)
        for kx in (2, 1, 3):
            cross[g, kx] = mail.post(out_a.at[kx, span], rxa.at[kx - 1, span], (row(kx, 0), gy))

    for d, h in long_way:
        post_b(d, h, 4)
    post_a(0)
    for d, h in short_way:
        post_b(d, h, 3)
    for g in range(1, ZS // GROUP):
        post_a(g)

    own_copy = pltpu.make_async_copy(own_par, all_par.at[gy], tab_sem.at[1])
    own_copy.start()
    par_mail = [mail.post(own_par, all_par.at[gy], device) for device in lanes]

    down = {}

    def settle_a(g):
        for kx in (1, 3, 2):
            cross[g, kx].wait_recv()
        for p in range(g * GROUP, (g + 1) * GROUP):
            total = (out_a[0, p].astype(F32) + rxa[0, p].astype(F32)
                     + rxa[1, p].astype(F32) + rxa[2, p].astype(F32))
            kz = ZS // 2 + p // 2 if p % 2 == 0 else ZS // 2 - 1 - p // 2
            if kz:
                sza[p] = total.astype(BF)
                down[p] = mail.post(sza.at[p], rza.at[p], (row(0, kz), gy))
            else:
                acc_a[...] = total

    for d, h in long_way:
        pass_b(d, h, 3)
    for d, h in short_way:
        pass_b(d, h, 2)
    settle_a(0)
    for d, h in long_way:
        pass_b(d, h, 2)
    settle_a(1)
    for d, h in short_way:
        pass_b(d, h, 1)
    settle_a(2)
    for d, h in long_way:
        pass_b(d, h, 1)
    settle_a(3)

    side = {}
    for h in (2, 1, 3, 0):
        for d in range(2):
            hop[d, h, 1].wait_recv()
        total = out_b[0, h].astype(F32) + rzb[0, h, 0].astype(F32) + rzb[1, h, 0].astype(F32)
        if h:
            sxb[h - 1] = total.astype(BF)
            side[h] = mail.post(sxb.at[h - 1], rxb.at[h - 1], (row(h, 0), gy))
        else:
            acc_b[...] = total

    in_s.wait()
    j = lax.broadcasted_iota(jnp.int32, (K, K), 0)
    l = lax.broadcasted_iota(jnp.int32, (K, K), 1)
    away = [lane(dy, 0) for dy in range(YS)]

    def finish(slot, total):
        rank = ranks_s[slot]
        merged = jnp.where((j < rank) & (l < rank), self_v[slot] + total, 0.0)
        gath[gy, slot] = merged.astype(BF)
        return [mail.post(gath.at[gy, slot], gath.at[gy, slot], device)
                for device in ((gx, away[2]), (gx, away[1]), (gx, away[3]), twin)]

    def forward(slot, sent):
        got = [sent[3]]
        for copy, source in ((sent[1], away[3]), (sent[2], away[1]), (sent[0], away[2])):
            copy.wait_recv()
            got.append(mail.post(gath.at[source, slot], gath.at[source, slot], twin))
        return got

    total = acc_a[...]
    for p in range(ZS - 1):
        down[p].wait_recv()
        total = total + rza[p].astype(F32)
    sent_a = finish(0, total)

    total = acc_b[...]
    for h in (1, 3, 2):
        side[h].wait_recv()
        total = total + rxb[h - 1].astype(F32)
    sent_b = finish(1, total)

    own_copy.wait()
    for copy in par_mail:
        copy.wait_recv()
    par_copy = pltpu.make_async_copy(all_par, par_tab, tab_sem.at[2])
    par_copy.start()

    got = forward(0, sent_a)
    got += forward(1, sent_b)
    par_copy.wait()

    first_row = gx * (YS * 2 * BOXES_HERE) + gy * BOXES_HERE
    found = []
    for q in range(BOXES_HERE):
        found_lane, found_slot = jnp.int32(0), jnp.int32(0)
        for k in range(YS * 2):
            for s in range(BOXES_HERE):
                hit = par_tab[k, s, 0] == first_row + q
                found_lane = jnp.where(hit, k, found_lane)
                found_slot = jnp.where(hit, s, found_slot)
        found.append((found_lane, found_slot))
    for copy in got:
        copy.wait_recv()
    for q in range(BOXES_HERE):
        out_ref[q] = gath[found[q][0], found[q][1]].astype(F32)
    for copy in mail.made:
        copy.wait_send()


def body(self_blk, near, back, interp, redinv, ranks, pivots, neighbors, parent):
    hbm = pl.BlockSpec(memory_space=pltpu.HBM)
    smem = pl.BlockSpec(memory_space=pltpu.SMEM)
    vmem = pl.BlockSpec(memory_space=pltpu.VMEM)
    blk = (K, K)
    return pl.pallas_call(
        kernel,
        out_shape=jax.ShapeDtypeStruct((BOXES_HERE, K, K), F32),
        in_specs=[hbm] * 5 + [smem, vmem, smem, smem],
        out_specs=vmem,
        scratch_shapes=[
            pltpu.VMEM((BOXES_HERE,) + blk, F32),
            pltpu.VMEM((BOXES_HERE, NBR, PTS, K), BF),
            pltpu.VMEM((BOXES_HERE, NBR, K, PTS), BF),
            pltpu.VMEM((BOXES_HERE, K, PTS), BF),
            pltpu.VMEM((BOXES_HERE, PTS, PTS), BF),
            pltpu.VMEM((BOXES_HERE, PTS, PTS), BF),
            pltpu.VMEM((ENTRIES + 1,) + blk, F32),
            pltpu.VMEM((BOXES_HERE, K), jnp.int32),
            pltpu.SMEM((BOXES_HERE, K), jnp.int32),
            pltpu.VMEM((BOXES_HERE, K), jnp.int32),
            pltpu.VMEM((YS * 2, BOXES_HERE, K), jnp.int32),
            pltpu.SMEM((YS * 2, BOXES_HERE, K), jnp.int32),
            pltpu.VMEM((XS, ZS) + blk, BF),
            pltpu.VMEM((ZS, XS) + blk, BF),
            pltpu.VMEM((XS - 1, ZS) + blk, BF),
            pltpu.VMEM((ZS - 1,) + blk, BF),
            pltpu.VMEM((ZS - 1,) + blk, BF),
            pltpu.VMEM(blk, F32),
            pltpu.VMEM((2, XS, ZS // 2) + blk, BF),
            pltpu.VMEM((XS - 1,) + blk, BF),
            pltpu.VMEM((XS - 1,) + blk, BF),
            pltpu.VMEM(blk, F32),
            pltpu.VMEM((YS * 2, BOXES_HERE) + blk, BF),
            pltpu.SemaphoreType.DMA((9,)),
            pltpu.SemaphoreType.DMA((3,)),
            pltpu.SemaphoreType.DMA((MESSAGES,)),
            pltpu.SemaphoreType.DMA((MESSAGES,)),
        ],
        compiler_params=pltpu.CompilerParams(
            collective_id=0, has_side_effects=True, vmem_limit_bytes=VMEM_LIMIT),
    )(self_blk, near, back, interp, redinv, ranks, pivots, neighbors, parent)


def solution(mesh):
    wide = ("gx", "gy")
    placed = (
        P(wide, None, None),
        P(wide, None, None, None),
        P(wide, None, None, None),
        P(wide, None, None),
        P(wide, None, None),
        P(wide),
        P(wide, None),
        P(wide, None),
        P(wide),
    )
    return jax.shard_map(
        body, mesh=mesh, in_specs=placed, out_specs=P(wide, None, None), check_vma=False
    )
```

time: 62.5 us -> 50.8 us (0.81)
  local copies, waits for them, and re-layouts: 8.44 us -> 1.57 us
  Pallas kernels: 53.8 us -> 49.1 us
    unnamed x17 -> x1, local copies, waits for them, and re-layouts: 8.44 us -> 1.57 us
    pallas_call x1, Pallas kernels: 53.8 us -> 49.1 us  [body(): pl.pallas_call(kernel, out_shape=jax.ShapeDtypeStruct((BOXES_HERE, K, K),...]
where the time goes in v2:
time: 50.8 us; the launch traced here: 50.7 us
  Pallas kernels  49.1 us (97%)
  local copies, waits for them, and re-layouts  1.57 us (3%)
    pallas_call x1, Pallas kernels, body(): pl.pallas_call(kernel, out_shape=jax.ShapeDtypeStruct((BOXES_HERE, K, K),...  49.1 us
    unnamed x1, local copies, waits for them, and re-layouts  1.57 us

profile of v2, /device:TPU:1, one launch (start us, length us, event | category | flops | bytes accessed | tf_op | source)
XLA Modules:
  0.0 50.7 jit_solution(18419016681580932395)
XLA Ops:
  0.0 49.1 %shard_map.91 = f32[2,128,128]{2,1,0:T(8,128)} custom-call(f32[2,128,128]{2,1,0:T(8,128)} %self_h.1, bf16[2,14,512,128]{3,2,1,0:T(8,128)(2,1)} %near_h.1, bf16[2,14,128,512]{3,2,1,0:T(8,128)(2,1)} %back_h.1, bf16[2,128,512]{2,1,0:T(8,128)(2,1)} %interp_h.1, bf16[2,512,512]{2,1,0:T(8,128)(2,1)} %redinv_h.1, s32[2]{0:T(128)} %ranks_s.1, s32[2,128]{1,0:T(2,128)} %pivots_v.1, ...), custom_call_target="tpu_custom_call" | custom-call | tf_op jit(solution)/shard_map/pallas_call | solution.py:286
  49.1 1.6 %copy.11 = f32[2,128,128]{2,1,0:T(8,128)} copy(f32[2,128,128]{2,1,0:T(8,128)} %shard_map.91) | data formatting | bytes 262144

commit v3 on v2

v3 whole, which is shorter than its diff:
```python
import jax
import jax.numpy as jnp
from jax import lax
from jax.experimental import pallas as pl
from jax.experimental.pallas import tpu as pltpu
from jax.sharding import PartitionSpec as P

BF = jnp.bfloat16
F32 = jnp.float32
MESH = pl.DeviceIdType.MESH
NT = (((1,), (1,)), ((), ()))

XS, ZS, YS = 4, 8, 4
BOXES_HERE, NBR, K, PTS = 2, 14, 128, 512
ENTRIES = BOXES_HERE * NBR
GROUP = 2
RB = 64
RA = K - RB
STEP = 7


class Mail:
    def __init__(self, send_sem, recv_sem):
        self.send_sem, self.recv_sem, self.made = send_sem, recv_sem, []

    def post(self, src, dst, device):
        m = len(self.made)
        copy = pltpu.make_async_remote_copy(
            src_ref=src, dst_ref=dst, send_sem=self.send_sem.at[m],
            recv_sem=self.recv_sem.at[m], device_id=device, device_id_type=MESH)
        copy.start()
        self.made.append(copy)
        return copy


MESSAGES = 96
VMEM_LIMIT = 62 << 20


def make_eliminator(rank, pivot_row, interp, redinv):
    point = lax.broadcasted_iota(jnp.int32, (PTS, K), 0)
    lane = lax.broadcasted_iota(jnp.int32, (PTS, K), 1)
    select_t = jnp.where((point == pivot_row) & (lane < rank), 1.0, 0.0).astype(F32)
    drop_col = (jnp.sum(select_t, axis=1, keepdims=True) - 1.0).astype(BF)
    select_t = select_t.astype(BF)
    taken = lax.dot_general(jnp.ones((8, K), BF), select_t, NT, preferred_element_type=F32)
    keep_row = (1.0 - taken[0:1]).astype(BF)
    living = jnp.where(lax.broadcasted_iota(jnp.int32, (K, 1), 0) < rank, 1.0, 0.0).astype(BF)
    coeff = interp * living * keep_row
    through = -lax.dot_general(redinv, coeff, NT, preferred_element_type=F32)
    spread = lax.dot_general(through.astype(BF), select_t, NT, preferred_element_type=F32)
    halfway = redinv * keep_row + spread.astype(BF)
    folded = jnp.dot(coeff, halfway, preferred_element_type=F32)
    placed = jnp.dot(select_t, folded.astype(BF), preferred_element_type=F32)
    return halfway * drop_col + placed.astype(BF)


def kernel(self_h, near_h, back_h, interp_h, redinv_h, ranks_h, pivots_h, nbr_h, par_h,
           out_ref,
           self_v, near_v, back_v, interp_v, redinv_v, elim_v, upd_a, upd_b, tab_v, tab_s,
           own_par, all_par, par_tab, ranks_s, pivots_v, nbr_s, par_s,
           out_a, out_b, rxa, sza, rza, acc_a, rzb, sxb, rxb, acc_b, gath_a, gath_b,
           load_sem, tab_sem, send_sem, recv_sem):
    gx, gy = lax.axis_index("gx"), lax.axis_index("gy")
    x, z = gx // ZS, gx % ZS
    y, c = gy // 2, gy % 2

    def row(dx, dz):
        return ((x + dx) % XS) * ZS + (z + dz) % ZS

    def lane(dy, dc):
        return ((y + dy) % YS) * 2 + (c + dc) % 2

    twin = (gx, lane(0, 1))
    lanes = [(gx, lane(dy, dc)) for dy in range(YS) for dc in range(2) if dy or dc]

    barrier = pltpu.get_barrier_semaphore()
    partners = ([(row(dx, 0), gy) for dx in range(1, XS)]
                + [(row(0, dz), gy) for dz in range(1, ZS)] + lanes)
    for device in partners:
        pl.semaphore_signal(barrier, inc=1, device_id=device, device_id_type=MESH)

    loads = []

    def load(src, dst):
        copy = pltpu.make_async_copy(src, dst, load_sem.at[len(loads)])
        copy.start()
        loads.append(copy)
        return copy

    in_small = [load(ranks_h, ranks_s), load(pivots_h, pivots_v), load(nbr_h, nbr_s),
                load(par_h, par_s)]
    in_i = [load(interp_h.at[b], interp_v.at[b]) for b in range(BOXES_HERE)]
    in_r = [load(redinv_h.at[b], redinv_v.at[b]) for b in range(BOXES_HERE)]
    in_low, in_n = [], []

    def load_box(b):
        in_low.append(load(back_h.at[b, :, pl.ds(0, RB)], back_v.at[b, :, pl.ds(0, RB)]))
        in_n.append(load(near_h.at[b], near_v.at[b]))


    in_small[0].wait()
    in_small[1].wait()
    upd_a[ENTRIES] = jnp.zeros((RA, K), F32)
    upd_b[ENTRIES] = jnp.zeros((RB, K), F32)

    for b in range(BOXES_HERE):
        in_i[b].wait()
        in_r[b].wait()
        load_box(b)
        elim_v[b] = make_eliminator(ranks_s[b], pivots_v[b:b + 1, :], interp_v[b], redinv_v[b])
    in_high = [load(back_h.at[b, :, pl.ds(RB, RA)], back_v.at[b, :, pl.ds(RB, RA)])
               for b in range(BOXES_HERE)]
    in_s = load(self_h, self_v)

    in_small[2].wait()
    in_small[3].wait()
    slots = lax.broadcasted_iota(jnp.int32, (1, K), 1)
    for b in range(BOXES_HERE):
        table = jnp.full((1, K), ENTRIES, jnp.int32)
        for n in range(NBR):
            target = nbr_s[b, n]
            slot = (target // (BOXES_HERE * YS * 2)) * BOXES_HERE + target % BOXES_HERE
            table = jnp.where(slots == slot, b * NBR + n, table)
        tab_v[b:b + 1, :] = table
    for b in range(BOXES_HERE):
        own_par[b:b + 1, :] = jnp.full((1, K), par_s[b], jnp.int32)
    tab_copy = pltpu.make_async_copy(tab_v, tab_s, tab_sem.at[0])
    tab_copy.start()
    own_copy = pltpu.make_async_copy(own_par, all_par.at[gy], tab_sem.at[1])
    own_copy.start()
    def products(upd, first, rows, needs):
        for b in range(BOXES_HERE):
            for copies in needs:
                copies[b].wait()

            def step(i, carry, b=b):
                wide = back_v[b, pl.ds(STEP * i, STEP), first:first + rows].reshape(STEP * rows, PTS)
                lifted = jnp.dot(wide, elim_v[b], preferred_element_type=F32).astype(BF)
                for h in range(STEP):
                    upd[b * NBR + STEP * i + h] = jnp.dot(
                        lifted[h * rows:(h + 1) * rows], near_v[b, STEP * i + h],
                        preferred_element_type=F32)
                return carry

            lax.fori_loop(0, NBR // STEP, step, 0)

    def order(p):
        return ZS // 2 + p // 2 if p % 2 == 0 else ZS // 2 - 1 - p // 2

    def gathered(upd, kx, kz):
        there = ((x + kx) % XS) * ZS + (z + kz) % ZS
        s = BOXES_HERE * there
        return [(upd[tab_s[0, s + q]] + upd[tab_s[1, s + q]]).astype(BF)
                for q in range(BOXES_HERE)]

    def assemble_b(*kzs):
        def one(kx, carry):
            for kz in kzs:
                for q, value in enumerate(gathered(upd_b, kx, kz)):
                    out_b[kz, kx, q] = value
            return carry

        lax.fori_loop(0, XS, one, 0)

    def assemble_a(g):
        def one(kx, carry):
            for p in range(g * GROUP, (g + 1) * GROUP):
                for q, value in enumerate(gathered(upd_a, kx, order(p))):
                    out_a[kx, p, q] = value
            return carry

        lax.fori_loop(0, XS, one, 0)

    mail = Mail(send_sem, recv_sem)

    hop = {}
    long_way = [(0, 0), (1, 2), (0, 1), (1, 3)]
    short_way = [(0, 2), (1, 0), (0, 3), (1, 1)]
    ways = [pair for both in zip(long_way, short_way) for pair in both]

    def toward(d, k):
        return k if d == 0 else ZS - k

    def post_b(d, h, k, links):
        hop[d, h, k] = mail.post(out_b.at[toward(d, k), h], rzb.at[d, h, k - 1],
                                 (row(0, toward(d, links)), gy))

    def pass_b(d, h, k):
        total = out_b[toward(d, k), h].astype(F32)
        if k == 2 and (d, h) in long_way:
            hop[d, h, 4].wait_recv()
            total = total + rzb[d, h, 3].astype(F32)
        hop[d, h, k + 1].wait_recv()
        out_b[toward(d, k), h] = (total + rzb[d, h, k].astype(F32)).astype(BF)
        post_b(d, h, k, 1)

    cross = {}

    def post_a(g):
        span = pl.ds(g * GROUP, GROUP)
        for kx in (2, 1, 3):
            cross[g, kx] = mail.post(out_a.at[kx, span], rxa.at[kx - 1, span], (row(kx, 0), gy))

    products(upd_b, 0, RB, (in_low, in_n))
    tab_copy.wait()
    assemble_b(4)
    pl.semaphore_wait(barrier, len(partners))
    for d, h in long_way:
        post_b(d, h, 4, 2)
    assemble_b(3, 5)
    for d, h in ways:
        post_b(d, h, 3, 1)
    assemble_b(2, 6)
    assemble_b(1, 7, 0)

    products(upd_a, RB, RA, (in_high,))
    for g in range(ZS // GROUP):
        assemble_a(g)
        post_a(g)
    par_mail = [mail.post(own_par, all_par.at[gy], device) for device in lanes]

    down = {}

    def settle_a(g):
        for kx in (1, 3, 2):
            cross[g, kx].wait_recv()
        for p in range(g * GROUP, (g + 1) * GROUP):
            total = (out_a[0, p].astype(F32) + rxa[0, p].astype(F32)
                     + rxa[1, p].astype(F32) + rxa[2, p].astype(F32))
            kz = order(p)
            if kz:
                sza[p] = total.astype(BF)
                down[p] = mail.post(sza.at[p], rza.at[p], (row(0, kz), gy))
            else:
                acc_a[...] = total

    for d, h in ways:
        pass_b(d, h, 2)
    for d, h in ways:
        pass_b(d, h, 1)
    settle_a(0)
    side = {}
    for h in (2, 1, 3, 0):
        for d in range(2):
            hop[d, h, 1].wait_recv()
        total = out_b[0, h].astype(F32) + rzb[0, h, 0].astype(F32) + rzb[1, h, 0].astype(F32)
        if h:
            sxb[h - 1] = total.astype(BF)
            side[h] = mail.post(sxb.at[h - 1], rxb.at[h - 1], (row(h, 0), gy))
        else:
            acc_b[...] = total
    settle_a(1)
    settle_a(2)
    settle_a(3)

    in_s.wait()
    away = [lane(dy, 0) for dy in range(YS)]

    def finish(gath, first, rows, total):
        j = lax.broadcasted_iota(jnp.int32, (rows, K), 0) + first
        l = lax.broadcasted_iota(jnp.int32, (rows, K), 1)
        for q in range(BOXES_HERE):
            rank = ranks_s[q]
            merged = jnp.where((j < rank) & (l < rank), self_v[q, first:first + rows] + total[q], 0.0)
            gath[gy, q] = merged.astype(BF)
        return [mail.post(gath.at[gy], gath.at[gy], device)
                for device in ((gx, away[2]), (gx, away[1]), (gx, away[3]), twin)]

    def forward(gath, sent):
        got = [sent[3]]
        for copy, source in ((sent[1], away[3]), (sent[2], away[1]), (sent[0], away[2])):
            copy.wait_recv()
            got.append(mail.post(gath.at[source], gath.at[source], twin))
        return got

    total = acc_b[...]
    for h in (1, 3, 2):
        side[h].wait_recv()
        total = total + rxb[h - 1].astype(F32)
    sent_b = finish(gath_b, 0, RB, total)

    total = acc_a[...]
    for p in range(ZS - 1):
        down[p].wait_recv()
        total = total + rza[p].astype(F32)
    sent_a = finish(gath_a, RB, RA, total)

    own_copy.wait()
    for copy in par_mail:
        copy.wait_recv()
    par_copy = pltpu.make_async_copy(all_par, par_tab, tab_sem.at[2])
    par_copy.start()

    got = forward(gath_b, sent_b)
    got += forward(gath_a, sent_a)
    par_copy.wait()

    first_row = gx * (YS * 2 * BOXES_HERE) + gy * BOXES_HERE
    found = []
    for q in range(BOXES_HERE):
        found_lane, found_slot = jnp.int32(0), jnp.int32(0)
        for k in range(YS * 2):
            for s in range(BOXES_HERE):
                hit = par_tab[k, s, 0] == first_row + q
                found_lane = jnp.where(hit, k, found_lane)
                found_slot = jnp.where(hit, s, found_slot)
        found.append((found_lane, found_slot))
    for copy in got:
        copy.wait_recv()
    for q in range(BOXES_HERE):
        out_ref[q, 0:RB] = gath_b[found[q][0], found[q][1]]
        out_ref[q, RB:K] = gath_a[found[q][0], found[q][1]]
    for copy in mail.made:
        copy.wait_send()


def body(self_blk, near, back, interp, redinv, ranks, pivots, neighbors, parent):
    hbm = pl.BlockSpec(memory_space=pl.ANY)
    a_blk, b_blk = (BOXES_HERE, RA, K), (BOXES_HERE, RB, K)
    rows = pl.pallas_call(
        kernel,
        out_shape=jax.ShapeDtypeStruct((BOXES_HERE, K, K), BF),
        in_specs=[hbm] * 9,
        out_specs=pl.BlockSpec(memory_space=pltpu.VMEM),
        scratch_shapes=[
            pltpu.VMEM((BOXES_HERE, K, K), F32),
            pltpu.VMEM((BOXES_HERE, NBR, PTS, K), BF),
            pltpu.VMEM((BOXES_HERE, NBR, K, PTS), BF),
            pltpu.VMEM((BOXES_HERE, K, PTS), BF),
            pltpu.VMEM((BOXES_HERE, PTS, PTS), BF),
            pltpu.VMEM((BOXES_HERE, PTS, PTS), BF),
            pltpu.VMEM((ENTRIES + 1, RA, K), F32),
            pltpu.VMEM((ENTRIES + 1, RB, K), F32),
            pltpu.VMEM((BOXES_HERE, K), jnp.int32),
            pltpu.SMEM((BOXES_HERE, K), jnp.int32),
            pltpu.VMEM((BOXES_HERE, K), jnp.int32),
            pltpu.VMEM((YS * 2, BOXES_HERE, K), jnp.int32),
            pltpu.SMEM((YS * 2, BOXES_HERE, K), jnp.int32),
            pltpu.SMEM((BOXES_HERE,), jnp.int32),
            pltpu.VMEM((BOXES_HERE, K), jnp.int32),
            pltpu.SMEM((BOXES_HERE, NBR), jnp.int32),
            pltpu.SMEM((BOXES_HERE,), jnp.int32),
            pltpu.VMEM((XS, ZS) + a_blk, BF),
            pltpu.VMEM((ZS, XS) + b_blk, BF),
            pltpu.VMEM((XS - 1, ZS) + a_blk, BF),
            pltpu.VMEM((ZS - 1,) + a_blk, BF),
            pltpu.VMEM((ZS - 1,) + a_blk, BF),
            pltpu.VMEM(a_blk, F32),
            pltpu.VMEM((2, XS, ZS // 2) + b_blk, BF),
            pltpu.VMEM((XS - 1,) + b_blk, BF),
            pltpu.VMEM((XS - 1,) + b_blk, BF),
            pltpu.VMEM(b_blk, F32),
            pltpu.VMEM((YS * 2,) + a_blk, BF),
            pltpu.VMEM((YS * 2,) + b_blk, BF),
            pltpu.SemaphoreType.DMA((15,)),
            pltpu.SemaphoreType.DMA((3,)),
            pltpu.SemaphoreType.DMA((MESSAGES,)),
            pltpu.SemaphoreType.DMA((MESSAGES,)),
        ],
        compiler_params=pltpu.CompilerParams(
            collective_id=0, has_side_effects=True, vmem_limit_bytes=VMEM_LIMIT),
    )(self_blk, near, back, interp, redinv, ranks, pivots, neighbors, parent)
    return rows.astype(F32)


def solution(mesh):
    wide = ("gx", "gy")
    placed = (
        P(wide, None, None),
        P(wide, None, None, None),
        P(wide, None, None, None),
        P(wide, None, None),
        P(wide, None, None),
        P(wide),
        P(wide, None),
        P(wide, None),
        P(wide),
    )
    return jax.shard_map(
        body, mesh=mesh, in_specs=placed, out_specs=P(wide, None, None), check_vma=False
    )
```

time: 50.8 us -> 44.2 us (0.87)
  Pallas kernels: 49.1 us -> 42.5 us
  local copies, waits for them, and re-layouts: 1.57 us -> 0 us
  other arithmetic: 0 us -> 1.5 us
    pallas_call x1, Pallas kernels: 49.1 us -> 42.5 us  [body(): pl.pallas_call(kernel, out_shape=jax.ShapeDtypeStruct((BOXES_HERE, K, K),...]
    unnamed x1 -> x0, local copies, waits for them, and re-layouts: 1.57 us -> none
    convert_element_type x0 -> x1, other arithmetic: none -> 1.5 us  [body(): return rows.astype(F32)]
where the time goes in v3:
time: 44.2 us; the launch traced here: 44 us
  Pallas kernels  42.5 us (96%)
  other arithmetic  1.5 us (3%)
    pallas_call x1, Pallas kernels, body(): pl.pallas_call(kernel, out_shape=jax.ShapeDtypeStruct((BOXES_HERE, K, K),...  42.5 us
    convert_element_type x1, other arithmetic, body(): return rows.astype(F32)  1.5 us

profile of v3, /device:TPU:1, one launch (start us, length us, event | category | flops | bytes accessed | tf_op | source)
XLA Modules:
  0.0 44.0 jit_solution(14204561916495453204)
XLA Ops:
  0.0 42.5 %shard_map.91 = bf16[2,128,128]{2,1,0:T(8,128)(2,1)} custom-call(f32[2,128,128]{2,1,0:T(8,128)} %self_h.1, bf16[2,14,512,128]{3,2,1,0:T(8,128)(2,1)} %near_h.1, bf16[2,14,128,512]{3,2,1,0:T(8,128)(2,1)} %back_h.1, bf16[2,128,512]{2,1,0:T(8,128)(2,1)} %interp_h.1, bf16[2,512,512]{2,1,0:T(8,128)(2,1)} %redinv_h.1, s32[2]{0:T(128)} %ranks_h.1, ...), custom_call_target="tpu_custom_call" | custom-call | tf_op jit(solution)/shard_map/pallas_call | solution.py:321
  42.5 1.5 %convert_element_type.3 = f32[2,128,128]{2,1,0:T(8,128)} convert(bf16[2,128,128]{2,1,0:T(8,128)(2,1)} %shard_map.91) | non-fusion elementwise | flops 32768 | bytes 196608 | tf_op jit(solution)/shard_map/convert_element_type | solution.py:364

commit v4 on v3

--- a/solution.py
+++ b/solution.py
@@ -16,7 +16,6 @@
 GROUP = 2
 RB = 64
 RA = K - RB
-STEP = 7
 
 
 class Mail:
@@ -37,7 +36,7 @@
 VMEM_LIMIT = 62 << 20
 
 
-def make_eliminator(rank, pivot_row, interp, redinv):
+def select_points(rank, pivot_row, interp):
     point = lax.broadcasted_iota(jnp.int32, (PTS, K), 0)
     lane = lax.broadcasted_iota(jnp.int32, (PTS, K), 1)
     select_t = jnp.where((point == pivot_row) & (lane < rank), 1.0, 0.0).astype(F32)
@@ -46,13 +45,22 @@
     taken = lax.dot_general(jnp.ones((8, K), BF), select_t, NT, preferred_element_type=F32)
     keep_row = (1.0 - taken[0:1]).astype(BF)
     living = jnp.where(lax.broadcasted_iota(jnp.int32, (K, 1), 0) < rank, 1.0, 0.0).astype(BF)
-    coeff = interp * living * keep_row
-    through = -lax.dot_general(redinv, coeff, NT, preferred_element_type=F32)
-    spread = lax.dot_general(through.astype(BF), select_t, NT, preferred_element_type=F32)
-    halfway = redinv * keep_row + spread.astype(BF)
-    folded = jnp.dot(coeff, halfway, preferred_element_type=F32)
-    placed = jnp.dot(select_t, folded.astype(BF), preferred_element_type=F32)
-    return halfway * drop_col + placed.astype(BF)
+    return select_t, drop_col, keep_row, interp * living * keep_row
+
+
+def make_eliminators(ranks_s, pivots_v, interp_v, redinv_v, elim_v):
+    boxes = range(BOXES_HERE)
+    select_t, drop_col, keep_row, coeff = zip(*[
+        select_points(ranks_s[b], pivots_v[b:b + 1, :], interp_v[b]) for b in boxes])
+    through = [(-lax.dot_general(redinv_v[b], coeff[b], NT, preferred_element_type=F32)).astype(BF)
+               for b in boxes]
+    spread = [lax.dot_general(through[b], select_t[b], NT, preferred_element_type=F32).astype(BF)
+              for b in boxes]
+    halfway = [redinv_v[b] * keep_row[b] + spread[b] for b in boxes]
+    folded = [jnp.dot(coeff[b], halfway[b], preferred_element_type=F32).astype(BF) for b in boxes]
+    placed = [jnp.dot(select_t[b], folded[b], preferred_element_type=F32).astype(BF) for b in boxes]
+    for b in boxes:
+        elim_v[b] = halfway[b] * drop_col[b] + placed[b]
 
 
 def kernel(self_h, near_h, back_h, interp_h, redinv_h, ranks_h, pivots_h, nbr_h, par_h,
@@ -74,24 +82,24 @@
     twin = (gx, lane(0, 1))
     lanes = [(gx, lane(dy, dc)) for dy in range(YS) for dc in range(2) if dy or dc]
 
+    loads = []
+
+    def load(src, dst):
+        copy = pltpu.make_async_copy(src, dst, load_sem.at[len(loads)])
+        copy.start()
+        loads.append(copy)
+        return copy
+
+    in_small = [load(ranks_h, ranks_s), load(pivots_h, pivots_v), load(nbr_h, nbr_s),
+                load(par_h, par_s)]
+    in_i = [load(interp_h.at[b], interp_v.at[b]) for b in range(BOXES_HERE)]
+    in_r = [load(redinv_h.at[b], redinv_v.at[b]) for b in range(BOXES_HERE)]
     barrier = pltpu.get_barrier_semaphore()
     partners = ([(row(dx, 0), gy) for dx in range(1, XS)]
                 + [(row(0, dz), gy) for dz in range(1, ZS)] + lanes)
     for device in partners:
         pl.semaphore_signal(barrier, inc=1, device_id=device, device_id_type=MESH)
 
-    loads = []
-
-    def load(src, dst):
-        copy = pltpu.make_async_copy(src, dst, load_sem.at[len(loads)])
-        copy.start()
-        loads.append(copy)
-        return copy
-
-    in_small = [load(ranks_h, ranks_s), load(pivots_h, pivots_v), load(nbr_h, nbr_s),
-                load(par_h, par_s)]
-    in_i = [load(interp_h.at[b], interp_v.at[b]) for b in range(BOXES_HERE)]
-    in_r = [load(redinv_h.at[b], redinv_v.at[b]) for b in range(BOXES_HERE)]
     in_low, in_n = [], []
 
     def load_box(b):
@@ -99,16 +107,16 @@
         in_n.append(load(near_h.at[b], near_v.at[b]))
 
 
+    load_box(0)
     in_small[0].wait()
     in_small[1].wait()
     upd_a[ENTRIES] = jnp.zeros((RA, K), F32)
     upd_b[ENTRIES] = jnp.zeros((RB, K), F32)
 
-    for b in range(BOXES_HERE):
-        in_i[b].wait()
-        in_r[b].wait()
-        load_box(b)
-        elim_v[b] = make_eliminator(ranks_s[b], pivots_v[b:b + 1, :], interp_v[b], redinv_v[b])
+    for copy in in_i + in_r:
+        copy.wait()
+    load_box(1)
+    make_eliminators(ranks_s, pivots_v, interp_v, redinv_v, elim_v)
     in_high = [load(back_h.at[b, :, pl.ds(RB, RA)], back_v.at[b, :, pl.ds(RB, RA)])
                for b in range(BOXES_HERE)]
     in_s = load(self_h, self_v)
@@ -134,16 +142,11 @@
             for copies in needs:
                 copies[b].wait()
 
-            def step(i, carry, b=b):
-                wide = back_v[b, pl.ds(STEP * i, STEP), first:first + rows].reshape(STEP * rows, PTS)
-                lifted = jnp.dot(wide, elim_v[b], preferred_element_type=F32).astype(BF)
-                for h in range(STEP):
-                    upd[b * NBR + STEP * i + h] = jnp.dot(
-                        lifted[h * rows:(h + 1) * rows], near_v[b, STEP * i + h],
-                        preferred_element_type=F32)
-                return carry
-
-            lax.fori_loop(0, NBR // STEP, step, 0)
+            wide = back_v[b, :, first:first + rows].reshape(NBR * rows, PTS)
+            lifted = jnp.dot(wide, elim_v[b], preferred_element_type=F32).astype(BF)
+            for n in range(NBR):
+                upd[b * NBR + n] = jnp.dot(lifted[n * rows:(n + 1) * rows], near_v[b, n],
+                                           preferred_element_type=F32)
 
     def order(p):
         return ZS // 2 + p // 2 if p % 2 == 0 else ZS // 2 - 1 - p // 2

time: 44.2 us -> 42 us (0.950)
  Pallas kernels: 42.5 us -> 40.3 us
    pallas_call x1, Pallas kernels: 42.5 us -> 40.3 us  [body(): pl.pallas_call(kernel, out_shape=jax.ShapeDtypeStruct((BOXES_HERE, K, K),...]
where the time goes in v4:
time: 42 us; the launch traced here: 41.9 us
  Pallas kernels  40.3 us (96%)
  other arithmetic  1.5 us (4%)
    pallas_call x1, Pallas kernels, body(): pl.pallas_call(kernel, out_shape=jax.ShapeDtypeStruct((BOXES_HERE, K, K),...  40.3 us
    convert_element_type x1, other arithmetic, body(): return rows.astype(F32)  1.5 us

profile of v4, /device:TPU:1, one launch (start us, length us, event | category | flops | bytes accessed | tf_op | source)
XLA Modules:
  0.0 41.9 jit_solution(750972374015451474)
XLA Ops:
  0.0 40.3 %shard_map.91 = bf16[2,128,128]{2,1,0:T(8,128)(2,1)} custom-call(f32[2,128,128]{2,1,0:T(8,128)} %self_h.1, bf16[2,14,512,128]{3,2,1,0:T(8,128)(2,1)} %near_h.1, bf16[2,14,128,512]{3,2,1,0:T(8,128)(2,1)} %back_h.1, bf16[2,128,512]{2,1,0:T(8,128)(2,1)} %interp_h.1, bf16[2,512,512]{2,1,0:T(8,128)(2,1)} %redinv_h.1, s32[2]{0:T(128)} %ranks_h.1, ...), custom_call_target="tpu_custom_call" | custom-call | tf_op jit(solution)/shard_map/pallas_call | solution.py:324
  40.4 1.5 %convert_element_type.3 = f32[2,128,128]{2,1,0:T(8,128)} convert(bf16[2,128,128]{2,1,0:T(8,128)(2,1)} %shard_map.91) | non-fusion elementwise | flops 32768 | bytes 196608 | tf_op jit(solution)/shard_map/convert_element_type | solution.py:367

commit v5 on v4

--- a/solution.py
+++ b/solution.py
@@ -258,8 +258,6 @@
     settle_a(3)
 
     in_s.wait()
-    away = [lane(dy, 0) for dy in range(YS)]
-
     def finish(gath, first, rows, total):
         j = lax.broadcasted_iota(jnp.int32, (rows, K), 0) + first
         l = lax.broadcasted_iota(jnp.int32, (rows, K), 1)
@@ -268,14 +266,8 @@
             merged = jnp.where((j < rank) & (l < rank), self_v[q, first:first + rows] + total[q], 0.0)
             gath[gy, q] = merged.astype(BF)
         return [mail.post(gath.at[gy], gath.at[gy], device)
-                for device in ((gx, away[2]), (gx, away[1]), (gx, away[3]), twin)]
-
-    def forward(gath, sent):
-        got = [sent[3]]
-        for copy, source in ((sent[1], away[3]), (sent[2], away[1]), (sent[0], away[2])):
-            copy.wait_recv()
-            got.append(mail.post(gath.at[source], gath.at[source], twin))
-        return got
+                for device in [(gx, lane(dy, dc)) for dy, dc in
+                               ((2, 1), (2, 0), (1, 1), (3, 1), (1, 0), (3, 0), (0, 1))]]
 
     total = acc_b[...]
     for h in (1, 3, 2):
@@ -295,8 +287,6 @@
     par_copy = pltpu.make_async_copy(all_par, par_tab, tab_sem.at[2])
     par_copy.start()
 
-    got = forward(gath_b, sent_b)
-    got += forward(gath_a, sent_a)
     par_copy.wait()
 
     first_row = gx * (YS * 2 * BOXES_HERE) + gy * BOXES_HERE
@@ -309,13 +299,13 @@
                 found_lane = jnp.where(hit, k, found_lane)
                 found_slot = jnp.where(hit, s, found_slot)
         found.append((found_lane, found_slot))
-    for copy in got:
+    for copy in mail.made:
+        copy.wait_send()
+    for copy in sent_b + sent_a:
         copy.wait_recv()
     for q in range(BOXES_HERE):
         out_ref[q, 0:RB] = gath_b[found[q][0], found[q][1]]
         out_ref[q, RB:K] = gath_a[found[q][0], found[q][1]]
-    for copy in mail.made:
-        copy.wait_send()
 
 
 def body(self_blk, near, back, interp, redinv, ranks, pivots, neighbors, parent):

time: 42 us -> 41.6 us (level)
  no operation moved by 1% of the time
where the time goes in v5:
time: 41.6 us; the launch traced here: 41.5 us
  Pallas kernels  39.9 us (96%)
  other arithmetic  1.5 us (4%)
    pallas_call x1, Pallas kernels, body(): pl.pallas_call(kernel, out_shape=jax.ShapeDtypeStruct((BOXES_HERE, K, K),...  39.9 us
    convert_element_type x1, other arithmetic, body(): return rows.astype(F32)  1.5 us

profile of v5, /device:TPU:1, one launch (start us, length us, event | category | flops | bytes accessed | tf_op | source)
XLA Modules:
  0.0 41.5 jit_solution(12644270534171223831)
XLA Ops:
  0.0 39.9 %shard_map.91 = bf16[2,128,128]{2,1,0:T(8,128)(2,1)} custom-call(f32[2,128,128]{2,1,0:T(8,128)} %self_h.1, bf16[2,14,512,128]{3,2,1,0:T(8,128)(2,1)} %near_h.1, bf16[2,14,128,512]{3,2,1,0:T(8,128)(2,1)} %back_h.1, bf16[2,128,512]{2,1,0:T(8,128)(2,1)} %interp_h.1, bf16[2,512,512]{2,1,0:T(8,128)(2,1)} %redinv_h.1, s32[2]{0:T(128)} %ranks_h.1, ...), custom_call_target="tpu_custom_call" | custom-call | tf_op jit(solution)/shard_map/pallas_call | solution.py:314
  39.9 1.5 %convert_element_type.3 = f32[2,128,128]{2,1,0:T(8,128)} convert(bf16[2,128,128]{2,1,0:T(8,128)(2,1)} %shard_map.91) | non-fusion elementwise | flops 32768 | bytes 196608 | tf_op jit(solution)/shard_map/convert_element_type | solution.py:357
